TPU v7x, 128 devices: a whole 4x4x4 slice. The times are simulated.
128 devices in a mesh: lat: 32 (over y, z, core), lev: 4 (over x).
Axes of the slice: x: 4, y: 4, z: 4, core: 2. Of those that a mesh axis runs over, the one named last changes fastest.
Arguments:
- probes: bfloat16 [512, 2, 256, 512], P('lat', None, None, 'lev'), may hold values from -40 to 40
- legendre: bfloat16 [512, 2, 512, 256], P('lat'), may hold values from -0.25 to 0.25
- quad_weight: float32 [512], P('lat'), may hold values from 0.5 to 2
- trunc_counts: int32 [512], P('lat'), may hold values from 128 to 512, as said below
- background: float32 [2, 512, 16, 1024], P(None, 'lat'), may hold values from 0.5 to 1.5
- level_up: float32 [16], replicated, may hold values from 0.2 to 0.5
- level_down: float32 [16], replicated, may hold values from 0.1 to 0.3
- viscosity: float32 [16], replicated, may hold values from 0.5 to 4
Outputs:
- basis_out: bfloat16 [512, 2, 256, 512], P('lat', None, None, 'lev')
- factor: float32 [16, 16], replicated
Inputs may be any that keep to these rules, and one draw needn't show every extreme that they name: `trunc_counts`: wavenumbers kept on a northern latitude and on its mirror; some latitude keeps all 512.
All inputs are finite; a program needn't handle non-finite values.
Results may differ from a plain program's by a relative error of at most 0.017.
Values may be sent and summed in bfloat16 or wider, within the bound.
No kernel may reach another device: no remote copies, remote signals or barrier semaphores. Data moves between devices by JAX's collectives and lax.ppermute only.
A program may use at most 128 MiB of HBM per device.

v0:
```python
import math
import jax
import jax.numpy as jnp
from jax import lax
from jax.sharding import PartitionSpec as P

M = 512
K = 512
PROBES = 16


def make_waves(wave_count, lon_count):
    zonal_ids = lax.broadcasted_iota(jnp.int32, (wave_count, lon_count), 0)
    lon_ids = lax.broadcasted_iota(jnp.int32, (wave_count, lon_count), 1)
    phase = (zonal_ids * lon_ids % lon_count).astype(jnp.float32) * (2.0 * math.pi / lon_count)
    return jnp.stack([jnp.cos(phase), -jnp.sin(phase)], axis=1).astype(jnp.bfloat16)


def damping(wave_first, wave_count, half_degree, visc_cols):
    zonal_ids = wave_first + jnp.arange(wave_count, dtype=jnp.int32)
    degree = (
        zonal_ids[:, None, None]
        + 2 * jnp.arange(half_degree, dtype=jnp.int32)[None, None, :]
        + jnp.arange(2, dtype=jnp.int32)[None, :, None]
    )
    scaled_deg = (degree * (degree + 1)).astype(jnp.float32) / float((M + K) * (M + K + 1))
    damp_one = 1.0 / (1.0 + scaled_deg[..., None] * visc_cols[None, None, None, :])
    return damp_one * damp_one


def unfold(parities):
    even_part = parities[:, 0].astype(jnp.float32)
    odd_part = parities[:, 1].astype(jnp.float32)
    return jnp.stack([even_part + odd_part, even_part - odd_part], axis=1)


def couple(grid_field, outer_coef, inner_coef, level_count, probe_count, reduce_levels):
    wave_count, _, row_count, col_count = grid_field.shape
    shaped = grid_field.reshape(wave_count, 2, row_count, level_count, 2, probe_count)
    level_total = reduce_levels(jnp.sum(shaped * inner_coef[:, None, None], axis=3))
    coupled = shaped + outer_coef[:, None, None] * level_total[:, :, :, None]
    return coupled.reshape(wave_count, 2, row_count, col_count)


def grid_pass(
    grid_field,
    wave_rows,
    gain_grid,
    keep_mask,
    weights,
    outer_coef,
    inner_coef,
    probe_count,
    promote,
    reduce_levels,
    adjoint,
):
    wave_count, _, row_count, col_count = grid_field.shape
    level_count = gain_grid.shape[2]
    if adjoint:
        grid_field = grid_field * weights[None, None, :, None]
    else:
        grid_field = couple(
            grid_field, outer_coef, inner_coef, level_count, probe_count, reduce_levels
        )
        grid_field = grid_field * keep_mask[:, None, :, None]
    operand = promote(grid_field.astype(jnp.bfloat16)).reshape(
        wave_count, 2, row_count, level_count, 2, probe_count
    )
    points = jnp.einsum(
        "mhjlcs,mci->hjlsi", operand, promote(wave_rows), preferred_element_type=jnp.float32
    )
    points = promote((points * gain_grid[:, :, :, None, :]).astype(jnp.bfloat16))
    analysed = jnp.einsum(
        "hjlsi,mci->mhjlcs", points, promote(wave_rows), preferred_element_type=jnp.float32
    )
    analysed = analysed.reshape(wave_count, 2, row_count, col_count)
    if adjoint:
        analysed = analysed * keep_mask[:, None, :, None]
        analysed = couple(analysed, outer_coef, inner_coef, level_count, probe_count, reduce_levels)
    else:
        analysed = analysed * weights[None, None, :, None]
    return jnp.stack(
        [analysed[:, 0] + analysed[:, 1], analysed[:, 0] - analysed[:, 1]], axis=1
    ).astype(jnp.bfloat16)


def to_parities(legendre, spectral):
    return jnp.einsum(
        "mpjq,mpqc->mpjc", legendre, spectral, preferred_element_type=jnp.float32
    ).astype(jnp.bfloat16)


def to_spectral(legendre, folded):
    return jnp.einsum("mpjq,mpjc->mpqc", legendre, folded, preferred_element_type=jnp.float32)


def same_values(values):
    return values


def level_sum(partial_value):
    return lax.psum(partial_value.astype(jnp.bfloat16), "lev").astype(jnp.float32)


def to_rows(parities):
    arrived = lax.all_to_all(parities, "lat", split_axis=2, concat_axis=0, tiled=True)
    return arrived


def to_waves(folded):
    arrived = lax.all_to_all(folded, "lat", split_axis=0, concat_axis=2, tiled=True)
    return arrived


def shards(
    probes, legendre, quad_weight, trunc_counts, background, level_up, level_down, viscosity
):
    lat_count = lax.axis_size("lat")
    lev_count = lax.axis_size("lev")
    lat_index = lax.axis_index("lat")
    lev_index = lax.axis_index("lev")
    wave_local = probes.shape[0]
    level_local = probes.shape[3] // (2 * PROBES)
    wave_count = wave_local * lat_count
    lon_count = 2 * wave_count
    wave_rows = make_waves(wave_count, lon_count)
    weights = quad_weight
    gain_grid = lax.dynamic_slice_in_dim(background, lev_index * level_local, level_local, 2)
    up_coef = lax.dynamic_slice_in_dim(level_up, lev_index * level_local, level_local, 0)
    down_coef = lax.dynamic_slice_in_dim(level_down, lev_index * level_local, level_local, 0)
    zonal_ids = jnp.arange(wave_count, dtype=jnp.int32)
    doubling = jnp.where(zonal_ids == 0, 1.0, 2.0).astype(jnp.float32)
    keep_mask = (zonal_ids[:, None] < trunc_counts[None, :]).astype(jnp.float32) * doubling[:, None]
    weights = weights / float(lon_count)
    grid_field = unfold(to_rows(to_parities(legendre, probes)))
    folded = grid_pass(
        grid_field,
        wave_rows,
        gain_grid,
        keep_mask,
        weights,
        up_coef,
        down_coef,
        PROBES,
        same_values,
        level_sum,
        False,
    )
    tangent = to_spectral(legendre, to_waves(folded))
    visc_cols = jnp.repeat(
        lax.dynamic_slice_in_dim(viscosity, lev_index * level_local, level_local, 0), 2 * PROBES
    )
    damping_sq = damping(lat_index * wave_local, wave_local, probes.shape[2], visc_cols)
    damped = (tangent * damping_sq).astype(jnp.bfloat16)
    grid_field = unfold(to_rows(to_parities(legendre, damped)))
    folded = grid_pass(
        grid_field,
        wave_rows,
        gain_grid,
        keep_mask,
        weights,
        down_coef,
        up_coef,
        PROBES,
        same_values,
        level_sum,
        True,
    )
    images = to_spectral(legendre, to_waves(folded))
    flattened = images.reshape(-1, PROBES)
    gram_local = lax.dot_general(
        flattened, flattened, (((0,), (0,)), ((), ())), precision=lax.Precision.HIGHEST
    )
    gram_matrix = lax.psum(gram_local, ("lat", "lev"))
    lower_factor = jnp.linalg.cholesky(gram_matrix)
    inverse = lax.linalg.triangular_solve(
        lower_factor, jnp.eye(PROBES, dtype=jnp.float32), left_side=True, lower=True
    )
    row_scale = math.sqrt(flattened.shape[0] * lat_count * lev_count)
    basis_out = (row_scale * jnp.dot(flattened, inverse.T, precision=lax.Precision.HIGHEST)).astype(
        jnp.bfloat16
    )
    basis_out = basis_out.reshape(images.shape)
    factor = lower_factor.T / row_scale
    return (basis_out, factor)


def solution(mesh):
    placed = (
        P("lat", None, None, "lev"),
        P("lat", None, None, None),
        P("lat"),
        P("lat"),
        P(None, "lat", None, None),
        P(),
        P(),
        P(),
    )
    return jax.shard_map(
        shards,
        mesh=mesh,
        in_specs=placed,
        out_specs=(P("lat", None, None, "lev"), P()),
        check_vma=False,
    )
```

profile of v0, /device:TPU:1, one launch (start us, length us, event | category | flops | bytes accessed | tf_op | source)
XLA Modules:
  0.0 726.1 jit_solution(6764757870753245017)
XLA Ops:
  7.2 1.6 copy-done
  8.8 5.7 convolution_convert_fusion
  14.5 6.3 copy.88
  20.8 9.8 %all-to-all-start = ((bf16[16,2,512,128]{3,1,0,2:T(2,128)(2,1)}), bf16[16,2,512,128]{3,1,0,2:T(2,128)(2,1)}, u32[]{:S(2)}, u32[]{:S(2)}) async-start(bf16[16,2,512,128]{3,1,0,2:T(2,128)(2,1)} %copy.88), calls=%async_computation | async-start | bytes 8388608 | tf_op jit(solution)/shard_map/all_to_all | solution.py:107
  31.0 51.7 %all-to-all-done = bf16[16,2,512,128]{3,1,0,2:T(2,128)(2,1)} async-done(((bf16[16,2,512,128]{3,1,0,2:T(2,128)(2,1)}), bf16[16,2,512,128]{3,1,0,2:T(2,128)(2,1)}, u32[]{:S(2)}, u32[]{:S(2)}) %all-to-all-start) | async-done | bytes 4194336 | tf_op jit(solution)/shard_map/all_to_all | solution.py:107
  82.7 3.8 copy.89
  87.7 3.8 convert_add_fusion.1
  91.5 5.3 copy.91
  96.8 5.3 copy.92
  102.1 5.5 multiply_reduce_fusion
  107.7 2.1 constant_dynamic-slice_fusion
  109.9 9.7 %negate_convert_fusion = (bf16[512,1,1024]{2,0,1:T(8,128)(2,1)S(1)}, bf16[512,1,1024]{2,0,1:T(8,128)(2,1)}) fusion(), kind=kLoop, calls=%fused_computation.52 | loop fusion | flops 8912896 | bytes 2097152 | tf_op jit(solution)/shard_map/convert.5
  119.6 33.0 %all-reduce.3.cloned.1.call-done = bf16[512,2,16,2,16]{0,4,2,1,3:T(8,128)(2,1)} async-done(((bf16[512,2,16,2,16]{0,4,2,1,3:T(8,128)(2,1)}), bf16[512,2,16,2,16]{0,4,2,1,3:T(8,128)(2,1)}) %all-reduce.3.cloned.1.call-update) | async-done | bytes 1048592 | tf_op jit(solution)/shard_map/psum | solution.py:103
  152.6 1.5 convert_element_type.94
  154.1 8.5 %fusion.14 = f32[2,16,4,16,1024,1]{4,3,0,2,1,5:T(8,128)S(1)} fusion(bf16[512,1,1024]{2,0,1:T(8,128)(2,1)S(1)} %get-tuple-element.24, bf16[512,1,1024]{2,0,1:T(8,128)(2,1)} %get-tuple-element.25, f32[512,16]{0,1:T(8,128)S(1)} %fusion.34, f32[512,2,16,2,16]{0,4,2,1,3:T(8,128)S(1)} %convert_element_type.94, f32[4]{0:T(128)S(1)} %dynamic_slice.12, ...), kind=kOutput, calls=%fused_computation.28 | convolution fusion | flops 4306501632 | bytes 21004304 | tf_op jit(solution)/shard_map/mhjlcs,mci->hjlsi/dot_general | solution.py:70
  162.6 4.6 fusion.19
  167.2 1.9 copy.95
  169.1 2.4 bitcast_multiply_fusion.2
  171.5 1.5 add_convert_fusion.1
  173.0 2.3 pad_maximum_fusion.1
  175.3 7.9 %copy.96 = bf16[512,2,16,128]{3,2,1,0:T(8,128)(2,1)} copy(bf16[512,2,16,128]{0,3,2,1:T(8,128)(2,1)} %pad_maximum_fusion.1) | data formatting | bytes 8388608 | tf_op jit(solution)/shard_map/stack | solution.py:83
  183.3 9.7 %all-to-all-start.1 = ((bf16[512,2,16,128]{3,2,1,0:T(8,128)(2,1)}), bf16[512,2,16,128]{3,2,1,0:T(8,128)(2,1)}, u32[]{:S(2)}, u32[]{:S(2)}) async-start(bf16[512,2,16,128]{3,2,1,0:T(8,128)(2,1)} %copy.96), calls=%async_computation.1 | async-start | bytes 8388608 | tf_op jit(solution)/shard_map/all_to_all | solution.py:112
  193.4 51.7 %all-to-all-done.1 = bf16[512,2,16,128]{3,2,1,0:T(8,128)(2,1)} async-done(((bf16[512,2,16,128]{3,2,1,0:T(8,128)(2,1)}), bf16[512,2,16,128]{3,2,1,0:T(8,128)(2,1)}, u32[]{:S(2)}, u32[]{:S(2)}) %all-to-all-start.1) | async-done | bytes 4194336 | tf_op jit(solution)/shard_map/all_to_all | solution.py:112
  245.1 5.3 copy.97
  250.4 13.1 %convert_bitcast_fusion = bf16[16,2,512,128]{2,3,1,0:T(8,128)(2,1)} fusion(bf16[16,2,512,256]{3,2,1,0:T(8,128)(2,1)} %param.9, bf16[16,2,512,128]{3,2,1,0:T(8,128)(2,1)} %bitcast.131, f32[128]{0:T(128)S(1)} %mul.211, f32[16,2,256]{2,1,0:T(2,128)S(1)} %fusion.33), kind=kOutput, calls=%fused_computation.33 | convolution fusion | flops 2155872256 | bytes 16810496 | tf_op jit(solution)/shard_map/mpjq,mpqc->mpjc/dot_general | solution.py:89
  263.5 11.2 %copy.99 = bf16[16,2,512,128]{3,1,0,2:T(2,128)(2,1)} copy(bf16[16,2,512,128]{2,3,1,0:T(8,128)(2,1)} %convert_bitcast_fusion) | data formatting | bytes 8388608 | tf_op jit(solution)/shard_map/convert_element_type | solution.py:91
  274.7 57.9 %all_to_all.72 = bf16[16,2,512,128]{3,1,0,2:T(2,128)(2,1)S(1)} all-to-all(bf16[16,2,512,128]{3,1,0,2:T(2,128)(2,1)} %copy.99), channel_id=1, replica_groups=mesh['lat'=32,'lev'=4] {'lat'}, dimensions={2} | all-to-all | bytes 8388608 | tf_op jit(solution)/shard_map/all_to_all | solution.py:107
  332.6 1.6 copy.100
  335.4 3.8 convert_add_fusion
  339.2 5.2 copy.102
  344.4 5.4 copy.103
  349.8 14.8 %fusion.2 = (bf16[512,2,16,2,16]{0,4,2,1,3:T(8,128)(2,1)}, f32[512,2,2,16,4,16]{0,5,4,3,2,1:T(8,128)}) fusion(f32[512,16]{0,1:T(8,128)S(1)} %fusion.34, f32[4]{0:T(128)S(1)} %dynamic_slice.12, f32[2,16,4,1024]{3,2,1,0:T(4,128)S(1)} %copy-done.5, bf16[512,1,1024]{2,0,1:T(8,128)(2,1)S(1)} %get-tuple-element.24, bf16[512,1,1024]{2,0,1:T(8,128)(2,1)S(1)} %copy-done.3, ...), kind=kOutput, calls=%fused_computation.7 | convolution fusion | flops 8611430400 | bytes 20480080 | tf_op jit(solution)/shard_map/hjlsi,mci->mhjlcs/dot_general | solution.py:74
  364.6 41.5 %all-reduce.5.cloned.1.call-done = bf16[512,2,16,2,16]{0,4,2,1,3:T(8,128)(2,1)} async-done(((bf16[512,2,16,2,16]{0,4,2,1,3:T(8,128)(2,1)}), bf16[512,2,16,2,16]{0,4,2,1,3:T(8,128)(2,1)}) %all-reduce.5.cloned.1.call-update) | async-done | bytes 1048592 | tf_op jit(solution)/shard_map/psum | solution.py:103
  406.1 1.5 convert_element_type.106
  407.6 5.2 bitcast_add_fusion
  412.9 4.2 copy.104
  417.1 4.8 add_convert_fusion
  421.9 2.3 pad_maximum_fusion.2
  424.2 7.9 %copy.105 = bf16[512,2,16,128]{3,2,1,0:T(8,128)(2,1)} copy(bf16[512,2,16,128]{0,3,2,1:T(8,128)(2,1)} %pad_maximum_fusion.2) | data formatting | bytes 8388608 | tf_op jit(solution)/shard_map/stack | solution.py:83
  432.1 60.4 %all_to_all.73 = bf16[512,2,16,128]{3,2,1,0:T(8,128)(2,1)S(1)} all-to-all(bf16[512,2,16,128]{3,2,1,0:T(8,128)(2,1)} %copy.105), channel_id=1, replica_groups=mesh['lat'=32,'lev'=4] {'lat'}, dimensions={0} | all-to-all | bytes 8388608 | tf_op jit(solution)/shard_map/all_to_all | solution.py:112
  494.7 3.5 convolution_bitcast_fusion
  498.2 5.4 copy.108
  503.6 19.6 %reshape.201 = f32[65536,16]{1,0:T(8,128)} reshape(f32[16,2,256,128]{3,2,1,0:T(8,128)} %copy.108) | data formatting | bytes 8388608 | tf_op jit(solution)/shard_map/reshape | solution.py:171
  523.2 64.4 %fusion.53 = f32[16,16]{0,1:T(8,128)S(1)} fusion(f32[65536,16]{1,0:T(8,128)} %reshape.201), kind=kOutput, calls=%fused_computation.82 | convolution fusion | flops 201326592 | bytes 4195328 | tf_op jit(solution)/shard_map/dot_general | solution.py:172
  587.5 63.6 %psum.23 = f32[16,16]{0,1:T(8,128)S(1)} all-reduce(f32[16,16]{0,1:T(8,128)S(1)} %fusion.53), channel_id=1, replica_groups=mesh['lat'=32,'lev'=4] {'lat','lev'}, use_global_device_ids=true, to_apply=%region_4.5 | all-reduce | flops 256 | bytes 2048 | tf_op jit(solution)/shard_map/psum | solution.py:175
  656.1 32.9 %fusion = bf16[65536,16]{0,1:T(8,128)(2,1)S(1)} fusion(f32[65536,16]{1,0:T(8,128)} %reshape.201, f32[16,16]{1,0:T(8,128)S(1)} %fusion.35), kind=kOutput, calls=%fused_computation.1 | convolution fusion | flops 203423744 | bytes 6292480 | tf_op jit(solution)/shard_map/dot_general | solution.py:181
  689.0 11.1 %copy.111 = bf16[65536,16]{1,0:T(8,128)(2,1)} copy(bf16[65536,16]{0,1:T(8,128)(2,1)S(1)} %fusion) | data formatting | bytes 4194304 | tf_op jit(solution)/shard_map/convert_element_type | solution.py:181
  700.1 18.9 %reshape.202 = bf16[16,2,256,128]{3,2,1,0:T(8,128)(2,1)} reshape(bf16[65536,16]{1,0:T(8,128)(2,1)} %copy.111) | data formatting | bytes 4194304 | tf_op jit(solution)/shard_map/reshape | solution.py:184
  (54 shorter events, 10.5 us)
Async XLA Ops:
  7.2 1.6 copy-start
  20.8 10.1 %copy-start.7 = (f32[16]{0:T(128)S(1)}, f32[16]{0:T(128)}, u32[]{:S(2)}) copy-start(f32[16]{0:T(128)} %param.14) | copy-start | bytes 196
  20.8 61.9 %all-to-all-start = ((bf16[16,2,512,128]{3,1,0,2:T(2,128)(2,1)}), bf16[16,2,512,128]{3,1,0,2:T(2,128)(2,1)}, u32[]{:S(2)}, u32[]{:S(2)}) async-start(bf16[16,2,512,128]{3,1,0,2:T(2,128)(2,1)} %copy.88), calls=%async_computation | async-start | bytes 8388608 | tf_op jit(solution)/shard_map/all_to_all | solution.py:107
  30.6 122.0 %all-reduce.3.cloned.1.call-start = ((), (), s32[]{:S(2)}) async-start(), calls=%async_computation.4 | async-start | bytes 2097152 | tf_op jit(solution)/shard_map/psum | solution.py:103
  102.1 5.5 copy-start.8
  102.1 7.7 %copy-start.9 = (f32[16]{0:T(128)S(1)}, f32[16]{0:T(128)}, u32[]{:S(2)}) copy-start(f32[16]{0:T(128)} %param.10) | copy-start | bytes 196
  102.1 7.8 %copy-start.6 = (s32[16]{0:T(128)S(1)}, s32[16]{0:T(128)}, u32[]{:S(2)}) copy-start(s32[16]{0:T(128)} %param.11) | copy-start | bytes 196
  154.1 8.5 %copy-start.2 = (bf16[512,1,1024]{2,0,1:T(8,128)(2,1)S(1)}, bf16[512,1,1024]{2,0,1:T(8,128)(2,1)}, u32[]{:S(2)}) copy-start(bf16[512,1,1024]{2,0,1:T(8,128)(2,1)} %get-tuple-element.25) | copy-start | bytes 3145732
  154.1 8.5 %copy-start.4 = (f32[2,16,4,1024]{3,2,1,0:T(4,128)S(1)}, f32[2,16,4,1024]{3,2,1,0:T(4,128)}, u32[]{:S(2)}) copy-start(f32[2,16,4,1024]{3,2,1,0:T(4,128)} %constant_dynamic-slice_fusion) | copy-start | bytes 1572868
  183.3 9.7 %copy-start.10 = (f32[16]{0:T(128)S(1)}, f32[16]{0:T(128)}, u32[]{:S(2)}) copy-start(f32[16]{0:T(128)} %param.15) | copy-start | bytes 196
  183.3 61.8 %all-to-all-start.1 = ((bf16[512,2,16,128]{3,2,1,0:T(8,128)(2,1)}), bf16[512,2,16,128]{3,2,1,0:T(8,128)(2,1)}, u32[]{:S(2)}, u32[]{:S(2)}) async-start(bf16[512,2,16,128]{3,2,1,0:T(8,128)(2,1)} %copy.96), calls=%async_computation.1 | async-start | bytes 8388608 | tf_op jit(solution)/shard_map/all_to_all | solution.py:112
  192.9 213.2 %all-reduce.5.cloned.1.call-start = ((), (), s32[]{:S(2)}) async-start(), calls=%async_computation.5 | async-start | bytes 2097152 | tf_op jit(solution)/shard_map/psum | solution.py:103
  344.4 5.4 copy-start.3
  344.4 5.4 copy-start.5
  432.1 61.6 %slice-start = ((s8[8388608]{0:T(1024)(128)(4,1)}), s8[4194304]{0:T(1024)(128)(4,1)S(1)}, s32[]{:S(2)}) async-start(s8[8388608]{0:T(1024)(128)(4,1)} %bitcast.116), calls=%async_computation.6 | async-start | bytes 8388608
  492.5 2.2 slice-start.1
  700.1 18.9 %copy-start.1 = (bf16[16,2,256,128]{3,2,1,0:T(8,128)(2,1)S(1)}, bf16[16,2,256,128]{3,2,1,0:T(8,128)(2,1)}, u32[]{:S(2)}) copy-start(bf16[16,2,256,128]{3,2,1,0:T(8,128)(2,1)} %param.8) | copy-start | bytes 6291460
Sparse Core Ops, SparseCore 0:
  107.7 44.8 all-reduce.2
  364.8 41.2 all-reduce.4
where the time goes:
time: 734 us; the launch traced here: 726 us
  blocking collectives  182 us (25%)
  waiting for transfers between devices  178 us (24%)
  matrix products  148 us (20%)
  local copies, waits for them, and re-layouts  136 us (19%)
  other arithmetic  48.5 us (7%)
  starting transfers between devices  19.8 us (3%)
  between operations  14.5 us (2%)
    psum x2, waiting for transfers between devices, level_sum(): lax.psum(partial_value.astype(jnp.bfloat16), 'lev').astype(jnp.float32)  74.4 us
    dot_general x1, matrix products, shards(): lax.dot_general(flattened, flattened, (((0,), (0,)), ((), ())), precision...  64.4 us
    psum x1, blocking collectives, shards(): gram_matrix = lax.psum(gram_local, ('lat', 'lev'))  63.6 us
    all_to_all x1, blocking collectives, to_waves(): lax.all_to_all(folded, 'lat', split_axis=0, concat_axis=2, tiled=True)  60.4 us
    all_to_all x1, blocking collectives, to_rows(): lax.all_to_all(parities, 'lat', split_axis=2, concat_axis=0, tiled=True)  57.9 us
    all_to_all x1, waiting for transfers between devices, to_waves(): lax.all_to_all(folded, 'lat', split_axis=0, concat_axis=2, tiled=True)  51.7 us
    all_to_all x1, waiting for transfers between devices, to_rows(): lax.all_to_all(parities, 'lat', split_axis=2, concat_axis=0, tiled=True)  51.7 us
    dot_general x1, matrix products, shards(): jnp.dot(flattened, inverse.T, precision=lax.Precision.HIGHEST)  32.9 us
  transfers between devices with their start and end apart: 4, of which 4 were waited for; matrix products, arithmetic and copies ran while one was open for 2% of the time, Pallas kernels for 0%

commit v1 on v0

--- a/solution.py
+++ b/solution.py
@@ -100,7 +100,9 @@
 
 
 def level_sum(partial_value):
-    return lax.psum(partial_value.astype(jnp.bfloat16), "lev").astype(jnp.float32)
+    return jnp.sum(lax.all_gather(partial_value.astype(jnp.bfloat16), "lev"), axis=0).astype(
+        jnp.float32
+    )
 
 
 def to_rows(parities):

time: 734 us -> 768 us (1.046)
  local copies, waits for them, and re-layouts: 136 us -> 155 us
  other arithmetic: 48.5 us -> 58.2 us
  waiting for transfers between devices: 178 us -> 186 us
    all_gather x0 -> x2, waiting for transfers between devices: none -> 82.2 us  [level_sum(): lax.all_gather(partial_value.astype(jnp.bfloat16), 'lev')]
    psum x2 -> x0, waiting for transfers between devices: 74.4 us -> none  [level_sum(): lax.psum(partial_value.astype(jnp.bfloat16), 'lev').astype(jnp.float32)]
    all_gather x0 -> x2, local copies, waits for them, and re-layouts: none -> 16.2 us  [level_sum(): lax.all_gather(partial_value.astype(jnp.bfloat16), 'lev')]
    reduce_sum x0 -> x2, other arithmetic: none -> 15.1 us  [level_sum(): jnp.sum(lax.all_gather(partial_value.astype(jnp.bfloat16), 'lev'), axis=0)]
    dot_general x1 -> x2, matrix products: 8.5 us -> 16.4 us  [grid_pass(): jnp.einsum('mhjlcs,mci->hjlsi', operand, promote(wave_rows), preferred_el...]
where the time goes in v1:
time: 768 us; the launch traced here: 759 us
  waiting for transfers between devices  186 us (24%)
  blocking collectives  180 us (23%)
  local copies, waits for them, and re-layouts  155 us (20%)
  matrix products  148 us (19%)
  other arithmetic  58.2 us (8%)
  starting transfers between devices  18.2 us (2%)
  between operations  14.8 us (2%)
    all_gather x2, waiting for transfers between devices, level_sum(): lax.all_gather(partial_value.astype(jnp.bfloat16), 'lev')  82.2 us
    dot_general x1, matrix products, shards(): lax.dot_general(flattened, flattened, (((0,), (0,)), ((), ())), precision...  64.1 us
    psum x1, blocking collectives, shards(): gram_matrix = lax.psum(gram_local, ('lat', 'lev'))  63.1 us
    all_to_all x1, blocking collectives, to_waves(): lax.all_to_all(folded, 'lat', split_axis=0, concat_axis=2, tiled=True)  58.7 us
    all_to_all x1, blocking collectives, to_rows(): lax.all_to_all(parities, 'lat', split_axis=2, concat_axis=0, tiled=True)  58.1 us
    all_to_all x1, waiting for transfers between devices, to_rows(): lax.all_to_all(parities, 'lat', split_axis=2, concat_axis=0, tiled=True)  51.8 us
    all_to_all x1, waiting for transfers between devices, to_waves(): lax.all_to_all(folded, 'lat', split_axis=0, concat_axis=2, tiled=True)  51.7 us
    dot_general x1, matrix products, shards(): jnp.dot(flattened, inverse.T, precision=lax.Precision.HIGHEST)  32.9 us
  transfers between devices with their start and end apart: 4, of which 4 were waited for; matrix products, arithmetic and copies ran while one was open for 2% of the time, Pallas kernels for 0%

profile of v1, /device:TPU:1, one launch (start us, length us, event | category | flops | bytes accessed | tf_op | source)
XLA Modules:
  0.0 759.4 jit_solution(6403282785535458303)
XLA Ops:
  8.8 5.7 convolution_convert_fusion
  14.5 6.3 copy.117
  20.8 9.8 %all-to-all-start = ((bf16[16,2,512,128]{3,1,0,2:T(2,128)(2,1)}), bf16[16,2,512,128]{3,1,0,2:T(2,128)(2,1)}, u32[]{:S(2)}, u32[]{:S(2)}) async-start(bf16[16,2,512,128]{3,1,0,2:T(2,128)(2,1)} %copy.117), calls=%async_computation | async-start | bytes 8388608 | tf_op jit(solution)/shard_map/all_to_all | solution.py:109
  30.9 51.8 %all-to-all-done = bf16[16,2,512,128]{3,1,0,2:T(2,128)(2,1)} async-done(((bf16[16,2,512,128]{3,1,0,2:T(2,128)(2,1)}), bf16[16,2,512,128]{3,1,0,2:T(2,128)(2,1)}, u32[]{:S(2)}, u32[]{:S(2)}) %all-to-all-start) | async-done | bytes 4194336 | tf_op jit(solution)/shard_map/all_to_all | solution.py:109
  82.7 3.8 copy.118
  87.7 3.8 convert_add_fusion.1
  91.5 5.3 copy.120
  96.8 5.3 copy.121
  102.1 4.5 multiply_reduce_fusion
  110.6 8.5 %negate_convert_fusion = (bf16[512,1,1024]{2,0,1:T(8,128)(2,1)S(1)}, bf16[512,1,1024]{2,0,1:T(8,128)(2,1)S(1)}) fusion(), kind=kLoop, calls=%fused_computation.52 | loop fusion | flops 8912896 | bytes 2097152 | tf_op jit(solution)/shard_map/convert.7
  119.1 37.5 %all-gather.5.cloned.1.call-done = bf16[2048,2,16,2,16]{0,4,3,2,1:T(8,128)(2,1)} async-done(((bf16[512,2,16,2,16]{0,4,3,2,1:T(8,128)(2,1)}), bf16[2048,2,16,2,16]{0,4,3,2,1:T(8,128)(2,1)}) %all-gather.5.cloned.1.call-update) | async-done | bytes 4194320 | tf_op jit(solution)/shard_map/all_gather | solution.py:103
  156.5 8.2 %reshape.223 = bf16[4,512,2,16,2,16]{1,0,5,4,3,2:T(4,128)(2,1)} reshape(bf16[2048,2,16,2,16]{0,4,3,2,1:T(8,128)(2,1)} %all-gather.5.cloned.1.call-done) | data formatting | bytes 8388608 | tf_op jit(solution)/shard_map/all_gather | solution.py:103
  164.8 7.6 reduce_sum.43
  172.3 8.3 %fusion.10 = f32[2,16,4,16,1024,1]{4,3,1,0,2,5:T(8,128)S(1)} fusion(bf16[512,1,1024]{2,0,1:T(8,128)(2,1)S(1)} %get-tuple-element.26, bf16[512,1,1024]{2,0,1:T(8,128)(2,1)S(1)} %get-tuple-element.27, f32[512,16]{0,1:T(8,128)S(1)} %fusion.33, f32[4]{0:T(128)S(1)} %dynamic_slice.12, bf16[512,2,16,2,16]{0,4,3,2,1:T(8,128)(2,1)S(1)} %reduce_sum.43, ...), kind=kOutput, calls=%fused_computation.27 | convolution fusion | flops 4306501632 | bytes 19955728 | tf_op jit(solution)/shard_map/mhjlcs,mci->hjlsi/dot_general | solution.py:70
  180.7 4.8 fusion.16
  185.5 1.9 copy.129
  187.4 2.2 bitcast_multiply_fusion.2
  191.1 2.3 pad_maximum_fusion.1
  193.4 7.9 %copy.130 = bf16[512,2,16,128]{3,2,1,0:T(8,128)(2,1)} copy(bf16[512,2,16,128]{0,3,2,1:T(8,128)(2,1)} %pad_maximum_fusion.1) | data formatting | bytes 8388608 | tf_op jit(solution)/shard_map/stack | solution.py:83
  201.4 8.1 %all-to-all-start.1 = ((bf16[512,2,16,128]{3,2,1,0:T(8,128)(2,1)}), bf16[512,2,16,128]{3,2,1,0:T(8,128)(2,1)}, u32[]{:S(2)}, u32[]{:S(2)}) async-start(bf16[512,2,16,128]{3,2,1,0:T(8,128)(2,1)} %copy.130), calls=%async_computation.1 | async-start | bytes 8388608 | tf_op jit(solution)/shard_map/all_to_all | solution.py:114
  209.9 51.7 %all-to-all-done.1 = bf16[512,2,16,128]{3,2,1,0:T(8,128)(2,1)} async-done(((bf16[512,2,16,128]{3,2,1,0:T(8,128)(2,1)}), bf16[512,2,16,128]{3,2,1,0:T(8,128)(2,1)}, u32[]{:S(2)}, u32[]{:S(2)}) %all-to-all-start.1) | async-done | bytes 4194336 | tf_op jit(solution)/shard_map/all_to_all | solution.py:114
  261.6 5.3 copy.131
  266.9 13.1 %convert_bitcast_fusion = bf16[16,2,512,128]{2,3,1,0:T(8,128)(2,1)} fusion(bf16[16,2,512,256]{3,2,1,0:T(8,128)(2,1)} %param.9, bf16[16,2,512,128]{3,2,1,0:T(8,128)(2,1)} %bitcast.124, f32[128]{0:T(128)S(1)} %mul.211, f32[16,2,256]{2,1,0:T(2,128)S(1)} %fusion.32), kind=kOutput, calls=%fused_computation.35 | convolution fusion | flops 2155872256 | bytes 16810496 | tf_op jit(solution)/shard_map/mpjq,mpqc->mpjc/dot_general | solution.py:89
  280.1 11.2 %copy.133 = bf16[16,2,512,128]{3,1,0,2:T(2,128)(2,1)} copy(bf16[16,2,512,128]{2,3,1,0:T(8,128)(2,1)} %convert_bitcast_fusion) | data formatting | bytes 8388608 | tf_op jit(solution)/shard_map/convert_element_type | solution.py:91
  291.3 58.1 %all_to_all.72 = bf16[16,2,512,128]{3,1,0,2:T(2,128)(2,1)S(1)} all-to-all(bf16[16,2,512,128]{3,1,0,2:T(2,128)(2,1)} %copy.133), channel_id=1, replica_groups=mesh['lat'=32,'lev'=4] {'lat'}, dimensions={2} | all-to-all | bytes 8388608 | tf_op jit(solution)/shard_map/all_to_all | solution.py:109
  349.4 1.6 copy.134
  352.2 3.8 convert_add_fusion
  356.0 5.3 copy.136
  361.3 5.4 copy.137
  366.7 8.1 %fusion.3 = bf16[2,16,4,16,1024]{4,3,0,2,1:T(8,128)(2,1)S(1)} fusion(f32[2,16,4,1024]{3,0,2,1:T(2,128)S(1)} %copy-done.5, bf16[512,1,1024]{2,0,1:T(8,128)(2,1)S(1)} %get-tuple-element.26, bf16[512,1,1024]{2,0,1:T(8,128)(2,1)S(1)} %copy-done.3, f32[512,1,16,4,2,16]{0,5,4,3,2,1:T(8,128)} %bitcast.123, f32[512,1,16,4,2,16]{0,5,4,3,2,1:T(8,128)} %bitcast.122, ...), kind=kOutput, calls=%fused_computation.9 | convolution fusion | flops 4306501632 | bytes 15204416 | tf_op jit(solution)/shard_map/mhjlcs,mci->hjlsi/dot_general | solution.py:70
  374.7 7.1 fusion.2
  382.9 44.7 %all-gather.7.cloned.1.call-done = bf16[2048,2,16,2,16]{0,4,3,2,1:T(8,128)(2,1)} async-done(((bf16[512,2,16,2,16]{0,4,3,2,1:T(8,128)(2,1)}), bf16[2048,2,16,2,16]{0,4,3,2,1:T(8,128)(2,1)}) %all-gather.7.cloned.1.call-update) | async-done | bytes 4194320 | tf_op jit(solution)/shard_map/all_gather | solution.py:103
  427.6 8.0 %reshape.224 = bf16[4,512,2,16,2,16]{1,0,5,4,3,2:T(4,128)(2,1)} reshape(bf16[2048,2,16,2,16]{0,4,3,2,1:T(8,128)(2,1)} %all-gather.7.cloned.1.call-done) | data formatting | bytes 8388608 | tf_op jit(solution)/shard_map/all_gather | solution.py:103
  435.6 7.6 reduce_sum.45
  443.2 5.0 bitcast_add_fusion
  448.2 4.3 copy.142
  452.5 4.8 add_convert_fusion
  457.3 2.3 pad_maximum_fusion.2
  459.7 7.9 %copy.143 = bf16[512,2,16,128]{3,2,1,0:T(8,128)(2,1)} copy(bf16[512,2,16,128]{0,3,2,1:T(8,128)(2,1)} %pad_maximum_fusion.2) | data formatting | bytes 8388608 | tf_op jit(solution)/shard_map/stack | solution.py:83
  467.6 58.7 %all_to_all.73 = bf16[512,2,16,128]{3,2,1,0:T(8,128)(2,1)S(1)} all-to-all(bf16[512,2,16,128]{3,2,1,0:T(8,128)(2,1)} %copy.143), channel_id=1, replica_groups=mesh['lat'=32,'lev'=4] {'lat'}, dimensions={0} | all-to-all | bytes 8388608 | tf_op jit(solution)/shard_map/all_to_all | solution.py:114
  528.5 3.5 convolution_bitcast_fusion
  532.0 5.4 copy.146
  537.4 19.6 %reshape.221 = f32[65536,16]{1,0:T(8,128)} reshape(f32[16,2,256,128]{3,2,1,0:T(8,128)} %copy.146) | data formatting | bytes 8388608 | tf_op jit(solution)/shard_map/reshape | solution.py:173
  557.0 64.1 %fusion.39 = f32[16,16]{0,1:T(8,128)S(1)} fusion(f32[65536,16]{1,0:T(8,128)} %reshape.221), kind=kOutput, calls=%fused_computation.81 | convolution fusion | flops 201326592 | bytes 4195328 | tf_op jit(solution)/shard_map/dot_general | solution.py:174
  621.1 63.1 %psum.7 = f32[16,16]{0,1:T(8,128)S(1)} all-reduce(f32[16,16]{0,1:T(8,128)S(1)} %fusion.39), channel_id=1, replica_groups=mesh['lat'=32,'lev'=4] {'lat','lev'}, use_global_device_ids=true, to_apply=%region_4.5 | all-reduce | flops 256 | bytes 2048 | tf_op jit(solution)/shard_map/psum | solution.py:177
  689.2 32.9 %fusion = bf16[65536,16]{0,1:T(8,128)(2,1)S(1)} fusion(f32[65536,16]{1,0:T(8,128)} %reshape.221, f32[16,16]{1,0:T(8,128)S(1)} %fusion.34), kind=kOutput, calls=%fused_computation.1 | convolution fusion | flops 203423744 | bytes 6292480 | tf_op jit(solution)/shard_map/dot_general | solution.py:183
  722.1 11.1 %copy.149 = bf16[65536,16]{1,0:T(8,128)(2,1)} copy(bf16[65536,16]{0,1:T(8,128)(2,1)S(1)} %fusion) | data formatting | bytes 4194304 | tf_op jit(solution)/shard_map/convert_element_type | solution.py:183
  733.2 18.9 %reshape.222 = bf16[16,2,256,128]{3,2,1,0:T(8,128)(2,1)} reshape(bf16[65536,16]{1,0:T(8,128)(2,1)} %copy.149) | data formatting | bytes 4194304 | tf_op jit(solution)/shard_map/reshape | solution.py:186
  (60 shorter events, 18.3 us)
Async XLA Ops:
  7.2 1.6 copy-start
  20.8 10.1 %copy-start.7 = (f32[16]{0:T(128)S(1)}, f32[16]{0:T(128)}, u32[]{:S(2)}) copy-start(f32[16]{0:T(128)} %param.14) | copy-start | bytes 196
  20.8 61.9 %all-to-all-start = ((bf16[16,2,512,128]{3,1,0,2:T(2,128)(2,1)}), bf16[16,2,512,128]{3,1,0,2:T(2,128)(2,1)}, u32[]{:S(2)}, u32[]{:S(2)}) async-start(bf16[16,2,512,128]{3,1,0,2:T(2,128)(2,1)} %copy.117), calls=%async_computation | async-start | bytes 8388608 | tf_op jit(solution)/shard_map/all_to_all | solution.py:109
  30.6 126.0 %all-gather.5.cloned.1.call-start = ((), (), s32[]{:S(2)}) async-start(), calls=%async_computation.4 | async-start | bytes 5242880 | tf_op jit(solution)/shard_map/all_gather | solution.py:103
  102.1 5.7 copy-start.8
  106.6 3.8 copy-start.9
  106.6 3.8 copy-start.6
  119.1 61.6 %copy-start.2 = (bf16[512,1,1024]{2,0,1:T(8,128)(2,1)}, bf16[512,1,1024]{2,0,1:T(8,128)(2,1)S(1)}, u32[]{:S(2)}) copy-start(bf16[512,1,1024]{2,0,1:T(8,128)(2,1)S(1)} %get-tuple-element.27) | copy-start | bytes 3145732
  172.3 8.4 %copy-start.4 = (f32[2,16,4,1024]{3,0,2,1:T(2,128)S(1)}, f32[2,16,4,1024]{3,0,2,1:T(2,128)}, u32[]{:S(2)}) copy-start(f32[2,16,4,1024]{3,0,2,1:T(2,128)} %copy.127) | copy-start | bytes 1572868
  201.4 8.2 %copy-start.10 = (f32[16]{0:T(128)S(1)}, f32[16]{0:T(128)}, u32[]{:S(2)}) copy-start(f32[16]{0:T(128)} %param.15) | copy-start | bytes 196
  201.4 60.2 %all-to-all-start.1 = ((bf16[512,2,16,128]{3,2,1,0:T(8,128)(2,1)}), bf16[512,2,16,128]{3,2,1,0:T(8,128)(2,1)}, u32[]{:S(2)}, u32[]{:S(2)}) async-start(bf16[512,2,16,128]{3,2,1,0:T(8,128)(2,1)} %copy.130), calls=%async_computation.1 | async-start | bytes 8388608 | tf_op jit(solution)/shard_map/all_to_all | solution.py:114
  209.5 218.2 %all-gather.7.cloned.1.call-start = ((), (), s32[]{:S(2)}) async-start(), calls=%async_computation.5 | async-start | bytes 5242880 | tf_op jit(solution)/shard_map/all_gather | solution.py:103
  361.3 5.4 copy-start.3
  361.3 5.4 copy-start.5
  467.6 59.9 %slice-start = ((s8[8388608]{0:T(1024)(128)(4,1)}), s8[4194304]{0:T(1024)(128)(4,1)S(1)}, s32[]{:S(2)}) async-start(s8[8388608]{0:T(1024)(128)(4,1)} %bitcast.109), calls=%async_computation.6 | async-start | bytes 8388608
  526.3 2.2 slice-start.1
  733.2 18.9 %copy-start.1 = (bf16[16,2,256,128]{3,2,1,0:T(8,128)(2,1)S(1)}, bf16[16,2,256,128]{3,2,1,0:T(8,128)(2,1)}, u32[]{:S(2)}) copy-start(bf16[16,2,256,128]{3,2,1,0:T(8,128)(2,1)} %param.8) | copy-start | bytes 6291460
Sparse Core Ops, SparseCore 0:
  107.9 48.5 all-gather.4
  383.0 44.5 all-gather.6
